TPU v7x, 32 devices: a whole 2x2x4 slice. The times are simulated.
32 devices in a mesh: freq: 4 (over x, core), rows: 8 (over z, y).
Axes of the slice: x: 2, y: 2, z: 4, core: 2. Of those that a mesh axis runs over, the one named last changes fastest.
Arguments:
- time_loads: float32 [256, 192, 2048], P('freq', None, 'rows'), may hold values from -6 to 6
- factor: float32 [16, 2, 2048, 2048], P('freq', None, 'rows'), may hold values from -0.09375 to 0.09375
- diag_inverse: float32 [16, 2, 2048, 256], P('freq', None, 'rows'), may hold values from -0.25 to 0.25
- pivot_order: int32 [8], replicated, may hold values from 0 to 7, each once
Outputs:
- solution: float32 [16, 2, 192, 2048], P('freq', None, None, 'rows')
Inputs may be any that keep to these rules, and one draw needn't show every extreme that they name: `pivot_order`: a permutation of the 8 row blocks.
All inputs are finite; a program needn't handle non-finite values.
Results may differ from a plain program's by a relative error of at most 0.0001.
Values sent between devices are 32-bit elements; how exact they have to be, the bound alone decides.
A program may use at most 128 MiB of HBM per device.

v0:
```python
import functools

import jax
import jax.numpy as jnp
from jax import lax
from jax.experimental import pallas as pl
from jax.experimental.pallas import tpu as pltpu
from jax.sharding import PartitionSpec as P

FREQS = 16
STEPS = 256
MESH = pl.DeviceIdType.MESH


def tables(count, length):
    freq_range = jnp.arange(count, dtype=jnp.float32)
    step_range = jnp.arange(length, dtype=jnp.float32)
    angles = 2.0 * jnp.pi * (freq_range[:, None] * step_range[None, :] % length) / length
    damping = jnp.exp(step_range * (jnp.log(0.1) / length))
    return (jnp.cos(angles) * damping[None, :], -jnp.sin(angles) * damping[None, :])


def zigzag(major, minor, extent):
    return minor + lax.rem(major, 2) * (extent - 1 - 2 * minor)


def chain_position(kind, index, outer, inner):
    z, y = lax.div(index, inner), lax.rem(index, inner)
    if kind == 1:
        y = inner - 1 - y
    if kind == 3:
        z = outer - 1 - z
    if kind < 2:
        return z * inner + zigzag(z, y, inner)
    return y * outer + zigzag(y, z, outer)


def chain_index(kind, position, outer, inner):
    if kind < 2:
        z = lax.div(position, inner)
        y = zigzag(z, lax.rem(position, inner), inner)
    else:
        y = lax.div(position, outer)
        z = zigzag(y, lax.rem(position, outer), outer)
    if kind == 1:
        y = inner - 1 - y
    if kind == 3:
        z = outer - 1 - z
    return z * inner + y


def split(value):
    high = value.astype(jnp.bfloat16)
    return high, (value - high.astype(jnp.float32)).astype(jnp.bfloat16)


def triple(value, right_high, right_low):
    high, low = split(value)
    count = value.shape[0]
    both = jnp.dot(
        jnp.concatenate([high, low], axis=0), right_high, preferred_element_type=jnp.float32
    )
    rest = jnp.dot(high, right_low, preferred_element_type=jnp.float32)
    return both[:count] + both[count:] + rest


def substitute(dims, pivot_ref, high_ref, low_ref, start_ref, out_ref, right_buf, left_buf,
               send_sem, recv_sem):
    freqs, blocks, units, cases, outer, inner = dims
    width = out_ref.shape[3]
    me = lax.axis_index("rows")
    slots = right_buf.shape[1]
    pieces = blocks * units
    last = blocks - 1

    barrier = pltpu.get_barrier_semaphore()
    for shift in range(1, blocks):
        pl.semaphore_signal(
            barrier, inc=1, device_id={"rows": lax.rem(me + shift, blocks)}, device_id_type=MESH
        )
    out_ref[...] = start_ref[...]
    pl.semaphore_wait(barrier, last)

    my_turn = jnp.int32(0)
    for turn in range(blocks):
        my_turn = my_turn + jnp.where(pivot_ref[turn] == me, turn, 0)

    def copy(direction, f, piece, target):
        buf = (right_buf, left_buf)[direction]
        slot = lax.rem(piece, slots)
        return pltpu.make_async_remote_copy(
            src_ref=buf.at[f, slot],
            dst_ref=buf.at[f, slot],
            send_sem=send_sem.at[direction, f, lax.rem(piece, 2)],
            recv_sem=recv_sem.at[direction, f, slot],
            device_id={"rows": target},
            device_id_type=MESH,
        )

    chains = []
    for f in range(freqs):
        kind = f % 4
        position = chain_position(kind, me, outer, inner)
        right = chain_index(kind, lax.rem(position + 1, blocks), outer, inner)
        left = chain_index(kind, lax.rem(position + last, blocks), outer, inner)
        chains.append((kind, position, right, left))

    def rows_of(piece):
        return pl.ds(pl.multiple_of(lax.rem(piece, units) * cases, 8), cases)

    def flow(direction, f, piece, target, is_first, is_last):
        buf = (right_buf, left_buf)[direction]
        slot = lax.rem(piece, slots)

        @pl.when((piece >= 0) & (piece < pieces))
        def _():
            @pl.when(jnp.logical_not(is_first))
            def _():
                copy(direction, f, piece, target).wait_recv()
                mine = pivot_ref[lax.div(piece, units)] == me
                buf[f, slot] = jnp.where(mine, out_ref[f, :, rows_of(piece), :], buf[f, slot])

            @pl.when(is_first)
            def _():
                buf[f, slot] = out_ref[f, :, rows_of(piece), :]

            @pl.when(jnp.logical_not(is_last))
            def _():
                @pl.when(piece >= 2)
                def _():
                    copy(direction, f, piece - 2, target).wait_send()

                copy(direction, f, piece, target).start()

    def finish(f, kind, position, piece):
        @pl.when((piece >= 0) & (piece < pieces))
        def _():
            turn = lax.div(piece, units)
            slot = lax.rem(piece, slots)
            owner = chain_position(kind, pivot_ref[turn], outer, inner)
            solved = jnp.where(owner <= position, right_buf[f, slot], left_buf[f, slot])
            turn_block = pivot_ref[turn]
            total = triple(
                solved.reshape(2 * cases, width), high_ref[turn_block, f], low_ref[turn_block, f]
            )
            from_real, from_imag = total[:cases], total[cases:]
            real = from_real[:, :width] - from_imag[:, width:]
            imag = from_real[:, width:] + from_imag[:, :width]
            rows = rows_of(piece)
            open_still = turn < my_turn
            real_now, imag_now = out_ref[f, 0, rows, :], out_ref[f, 1, rows, :]
            out_ref[f, 0, rows, :] = jnp.where(open_still, real_now - real, real_now)
            out_ref[f, 1, rows, :] = jnp.where(open_still, imag_now - imag, imag_now)

    def tick(t, carry):
        for f, (kind, position, right, left) in enumerate(chains):
            at_start, at_end = position == 0, position == last
            flow(0, f, t - position, right, at_start, at_end)
            flow(1, f, t - (last - position), left, at_end, at_start)
            finish(f, kind, position, t - jnp.maximum(position, last - position))
        return carry

    lax.fori_loop(0, pieces + last, tick, 0)

    for f, (kind, position, right, left) in enumerate(chains):
        for piece in (pieces - 2, pieces - 1):
            @pl.when(position < last)
            def _():
                copy(0, f, jnp.int32(piece), right).wait_send()

            @pl.when(position > 0)
            def _():
                copy(1, f, jnp.int32(piece), left).wait_send()


def exchange(dims, spectra_ref, inverse_high, inverse_low, factor_ref, high_ref, low_ref,
             start_ref, core_buf, chip_buf, core_send, core_recv, chip_send, chip_recv):
    freqs, blocks, chips = dims
    cases, width = start_ref.shape[2], start_ref.shape[3]
    me = lax.axis_index("freq")
    chip, core = lax.div(me, 2), lax.rem(me, 2)
    step = pl.program_id(0) * blocks + pl.program_id(1)
    steps = freqs * blocks

    def core_copy(to_chip, f):
        return pltpu.make_async_remote_copy(
            src_ref=spectra_ref.at[to_chip * 2 + 1 - core, f],
            dst_ref=core_buf.at[to_chip, f],
            send_sem=core_send.at[to_chip, f],
            recv_sem=core_recv.at[to_chip, f],
            device_id={"freq": chip * 2 + 1 - core},
            device_id_type=MESH,
        )

    def chip_copy(shift, f):
        to_chip = lax.rem(chip + shift, chips)
        slot = chips - 1 - shift
        return pltpu.make_async_remote_copy(
            src_ref=core_buf.at[to_chip, f],
            dst_ref=chip_buf.at[slot, f],
            send_sem=chip_send.at[slot, f],
            recv_sem=chip_recv.at[slot, f],
            device_id={"freq": to_chip * 2 + core},
            device_id_type=MESH,
        )

    @pl.when(step == 0)
    def _():
        barrier = pltpu.get_barrier_semaphore()
        pl.semaphore_signal(
            barrier, inc=1, device_id={"freq": chip * 2 + 1 - core}, device_id_type=MESH
        )
        for shift in range(1, chips):
            pl.semaphore_signal(
                barrier, inc=1, device_id={"freq": lax.rem(chip + shift, chips) * 2 + core},
                device_id_type=MESH,
            )
        pl.semaphore_wait(barrier, chips)
        for f in range(freqs):
            for shift in range(1, chips + 1):
                core_copy(lax.rem(chip + shift, chips), f).start()

    for f in range(freqs):
        @pl.when(step == 1 + f)
        def _():
            for shift in range(1, chips):
                to_chip = lax.rem(chip + shift, chips)
                core_copy(to_chip, f).wait_recv()
                core_buf[to_chip, f] = core_buf[to_chip, f] + spectra_ref[to_chip * 2 + core, f]
                chip_copy(shift, f).start()

    taken = factor_ref[0]
    turned = jnp.concatenate([taken[0].T, taken[1].T], axis=0)
    f_now = pl.program_id(0)
    total = triple(turned, inverse_high[f_now], inverse_low[f_now])
    from_real, from_imag = total[:width], total[width:]
    real = from_real[:, :width] - from_imag[:, width:]
    imag = from_real[:, width:] + from_imag[:, :width]
    high_ref[0, 0], low_ref[0, 0] = split(jnp.concatenate([real, imag], axis=1))

    for f in range(freqs):
        @pl.when(step == steps - freqs + f)
        def _():
            core_copy(chip, f).wait_recv()
            value = spectra_ref[me, f] + core_buf[chip, f]
            for shift in range(1, chips):
                chip_copy(shift, f).wait_recv()
                value = value + chip_buf[chips - 1 - shift, f]
            solved = triple(value.reshape(2 * cases, width), inverse_high[f], inverse_low[f])
            start_ref[f, 0] = solved[:cases, :width] - solved[cases:, width:]
            start_ref[f, 1] = solved[:cases, width:] + solved[cases:, :width]
            for to_chip in range(chips):
                core_copy(to_chip, f).wait_send()
            for shift in range(1, chips):
                chip_copy(shift, f).wait_send()


def body(time_loads, factor, diag_inverse, pivot_order):
    high = lax.Precision.HIGH
    local_freqs = factor.shape[0]
    local_steps = time_loads.shape[0]
    all_cases = time_loads.shape[1]
    blocks = lax.axis_size("rows")
    owners = lax.axis_size("freq")
    width = diag_inverse.shape[3]
    cosine_table, sine_table = tables(FREQS, STEPS)
    table = jnp.stack([cosine_table, sine_table], axis=1)
    offset = lax.axis_index("freq") * local_steps
    part = lax.dynamic_slice_in_dim(table, offset, local_steps, 2)
    part = part.reshape(-1, local_steps)
    spectra = jnp.einsum("gn,ncr->gcr", part, time_loads, precision=high)
    spectra = spectra.reshape(owners, local_freqs, 2, all_cases, width)

    inverse = jnp.concatenate(
        [diag_inverse[:, 0].swapaxes(1, 2), diag_inverse[:, 1].swapaxes(1, 2)], axis=2
    )
    rounded = lax.reduce_precision(inverse, 8, 7)
    inverse_high = rounded.astype(jnp.bfloat16)
    inverse_low = (inverse - rounded).astype(jnp.bfloat16)

    chips = owners // 2
    vmem = pl.BlockSpec(memory_space=pltpu.VMEM)
    block = pl.BlockSpec((1, 1, width, 2 * width), lambda f, k: (k, f, 0, 0))
    scaled = jax.ShapeDtypeStruct((blocks, local_freqs, width, 2 * width), jnp.bfloat16)
    scaled_high, scaled_low, start = pl.pallas_call(
        functools.partial(exchange, (local_freqs, blocks, chips)),
        grid=(local_freqs, blocks),
        out_shape=(
            scaled, scaled,
            jax.ShapeDtypeStruct((local_freqs, 2, all_cases, width), jnp.float32),
        ),
        in_specs=[
            vmem, vmem, vmem,
            pl.BlockSpec((1, 2, width, width), lambda f, k: (f, 0, 0, k)),
        ],
        out_specs=(block, block, vmem),
        scratch_shapes=[
            pltpu.VMEM((chips, local_freqs, 2, all_cases, width), jnp.float32),
            pltpu.VMEM((max(chips - 1, 1), local_freqs, 2, all_cases, width), jnp.float32),
            pltpu.SemaphoreType.DMA((chips, local_freqs)),
            pltpu.SemaphoreType.DMA((chips, local_freqs)),
            pltpu.SemaphoreType.DMA((max(chips - 1, 1), local_freqs)),
            pltpu.SemaphoreType.DMA((max(chips - 1, 1), local_freqs)),
        ],
        compiler_params=pltpu.CompilerParams(
            collective_id=1, has_side_effects=True, vmem_limit_bytes=60 * 1024 * 1024,
            dimension_semantics=("arbitrary", "arbitrary"),
        ),
    )(spectra, inverse_high, inverse_low, factor)

    units = blocks
    cases = -(-all_cases // (8 * units)) * 8
    padded = cases * units
    if padded > all_cases:
        start = jnp.pad(start, ((0, 0), (0, 0), (0, padded - all_cases), (0, 0)))
    inner = 1
    while 4 * inner * inner <= blocks:
        inner *= 2
    slots = 2 * units
    dims = (local_freqs, blocks, units, cases, blocks // inner, inner)
    solution = pl.pallas_call(
        functools.partial(substitute, dims),
        out_shape=jax.ShapeDtypeStruct(start.shape, jnp.float32),
        in_specs=[pl.BlockSpec(memory_space=pltpu.SMEM), vmem, vmem, vmem],
        out_specs=vmem,
        scratch_shapes=[
            pltpu.VMEM((local_freqs, slots, 2, cases, width), jnp.float32),
            pltpu.VMEM((local_freqs, slots, 2, cases, width), jnp.float32),
            pltpu.SemaphoreType.DMA((2, local_freqs, 2)),
            pltpu.SemaphoreType.DMA((2, local_freqs, slots)),
        ],
        compiler_params=pltpu.CompilerParams(
            collective_id=0, has_side_effects=True, vmem_limit_bytes=60 * 1024 * 1024
        ),
    )(pivot_order, scaled_high, scaled_low, start)
    return solution[:, :, :all_cases]


def solution(mesh):
    placed = (
        P("freq", None, "rows"),
        P("freq", None, "rows", None),
        P("freq", None, "rows", None),
        P(),
    )
    return jax.shard_map(
        body, mesh=mesh, in_specs=placed, out_specs=P("freq", None, None, "rows"), check_vma=False
    )
```

profile of v0, /device:TPU:0, one launch (start us, length us, event | category | flops | bytes accessed | tf_op | source)
XLA Modules:
  0.0 333.3 jit_solution(16717629628386400450)
XLA Ops:
  0.0 0.1 negate_multiply_fusion
  0.1 0.1 fusion.4
  0.2 1.7 fusion.9
  1.9 0.3 copy.20
  2.2 0.3 copy.21
  2.6 1.6 fusion.2
  4.2 16.6 %fusion = f32[4,4,2,192,256]{4,1,3,2,0:T(4,128)S(1)} fusion(f32[64,192,256,1,1]{2,1,0,4,3:T(8,128)} %bitcast.13, f32[4,4,2,64,1]{3,1,0,2,4:T(4,128)S(1)} %bitcast.12), kind=kOutput, calls=%fused_computation | convolution fusion | flops 603979776 | bytes 18882560 | tf_op jit(solution)/shard_map/gn,ncr->gcr/dot_general | solution.py:271
  20.8 3.8 %copy.13.spectra_ref = f32[4,4,2,192,256]{4,3,2,1,0:T(8,128)} copy(f32[4,4,2,192,256]{4,1,3,2,0:T(4,128)S(1)} %fusion) | data formatting | bytes 12582912 | tf_op jit(solution)/shard_map/gn,ncr->gcr/dot_general | solution.py:271
  24.5 44.8 %shard_map.46 = (bf16[8,4,256,512]{3,2,1,0:T(8,128)(2,1)}, bf16[8,4,256,512]{3,2,1,0:T(8,128)(2,1)}, f32[4,2,192,256]{3,2,1,0:T(8,128)}) custom-call(f32[4,4,2,192,256]{4,3,2,1,0:T(8,128)} %copy.13.spectra_ref, bf16[4,256,512]{2,1,0:T(8,128)(2,1)} %get-tuple-element.12.inverse_high, bf16[4,256,512]{2,1,0:T(8,128)(2,1)} %get-tuple-element.11.inverse_low, ...), custom_call_target="tpu_custom_call" | custom-call | tf_op jit(solution)/shard_map/pallas_call | solution.py:285
  69.4 261.3 %shard_map.47 = f32[4,2,192,256]{3,2,1,0:T(8,128)} custom-call(s32[8]{0:T(128)} %pivot_ref.1, bf16[8,4,256,512]{3,2,1,0:T(8,128)(2,1)} %get-tuple-element.8.high_ref, bf16[8,4,256,512]{3,2,1,0:T(8,128)(2,1)} %get-tuple-element.9.low_ref, f32[4,2,192,256]{3,2,1,0:T(8,128)} %get-tuple-element.10.start_ref), custom_call_target="tpu_custom_call" | custom-call | tf_op jit(solution)/shard_map/pallas_call | solution.py:321
  330.7 2.7 copy.27
  (1 shorter events, 0.0 us)
where the time goes:
time: 334 us; the launch traced here: 333 us
  Pallas kernels  306 us (92%)
  matrix products  16.6 us (5%)
  local copies, waits for them, and re-layouts  8.74 us (3%)
    pallas_call x1, Pallas kernels, body(): pl.pallas_call(functools.partial(substitute, dims), out_shape=jax.ShapeDt...  261 us
    pallas_call x1, Pallas kernels, body(): pl.pallas_call(functools.partial(exchange, (local_freqs, blocks, chips)),...  44.8 us
    dot_general x1, matrix products, body(): spectra = jnp.einsum('gn,ncr->gcr', part, time_loads, precision=high)  16.6 us

commit v1 on v0

--- a/solution.py
+++ b/solution.py
@@ -70,8 +70,8 @@
     width = out_ref.shape[3]
     me = lax.axis_index("rows")
     slots = right_buf.shape[1]
-    pieces = blocks * units
     last = blocks - 1
+    pieces = last * units
 
     barrier = pltpu.get_barrier_semaphore()
     for shift in range(1, blocks):
@@ -308,15 +308,17 @@
         ),
     )(spectra, inverse_high, inverse_low, factor)
 
-    units = blocks
-    cases = -(-all_cases // (8 * units)) * 8
+    cases = 8
+    while -(-all_cases // (cases + 8)) >= blocks:
+        cases += 8
+    units = -(-all_cases // cases)
     padded = cases * units
     if padded > all_cases:
         start = jnp.pad(start, ((0, 0), (0, 0), (0, padded - all_cases), (0, 0)))
     inner = 1
     while 4 * inner * inner <= blocks:
         inner *= 2
-    slots = 2 * units
+    slots = 2 * blocks
     dims = (local_freqs, blocks, units, cases, blocks // inner, inner)
     solution = pl.pallas_call(
         functools.partial(substitute, dims),

time: 334 us -> 305 us (0.913)
  Pallas kernels: 306 us -> 277 us
    pallas_call x1, Pallas kernels: 261 us -> 232 us  [body(): pl.pallas_call(functools.partial(substitute, dims), out_shape=jax.ShapeDt...]
where the time goes in v1:
time: 305 us; the launch traced here: 304 us
  Pallas kernels  277 us (91%)
  matrix products  16.6 us (5%)
  local copies, waits for them, and re-layouts  8.74 us (3%)
    pallas_call x1, Pallas kernels, body(): pl.pallas_call(functools.partial(substitute, dims), out_shape=jax.ShapeDt...  232 us
    pallas_call x1, Pallas kernels, body(): pl.pallas_call(functools.partial(exchange, (local_freqs, blocks, chips)),...  44.8 us
    dot_general x1, matrix products, body(): spectra = jnp.einsum('gn,ncr->gcr', part, time_loads, precision=high)  16.6 us

profile of v1, /device:TPU:0, one launch (start us, length us, event | category | flops | bytes accessed | tf_op | source)
XLA Modules:
  0.0 304.5 jit_solution(14796817487886061784)
XLA Ops:
  0.0 0.1 negate_multiply_fusion
  0.1 0.1 fusion.4
  0.2 1.7 fusion.9
  1.9 0.3 copy.20
  2.2 0.3 copy.21
  2.6 1.6 fusion.2
  4.2 16.6 %fusion = f32[4,4,2,192,256]{4,1,3,2,0:T(4,128)S(1)} fusion(f32[64,192,256,1,1]{2,1,0,4,3:T(8,128)} %bitcast.13, f32[4,4,2,64,1]{3,1,0,2,4:T(4,128)S(1)} %bitcast.12), kind=kOutput, calls=%fused_computation | convolution fusion | flops 603979776 | bytes 18882560 | tf_op jit(solution)/shard_map/gn,ncr->gcr/dot_general | solution.py:271
  20.8 3.8 %copy.13.spectra_ref = f32[4,4,2,192,256]{4,3,2,1,0:T(8,128)} copy(f32[4,4,2,192,256]{4,1,3,2,0:T(4,128)S(1)} %fusion) | data formatting | bytes 12582912 | tf_op jit(solution)/shard_map/gn,ncr->gcr/dot_general | solution.py:271
  24.5 44.8 %shard_map.46 = (bf16[8,4,256,512]{3,2,1,0:T(8,128)(2,1)}, bf16[8,4,256,512]{3,2,1,0:T(8,128)(2,1)}, f32[4,2,192,256]{3,2,1,0:T(8,128)}) custom-call(f32[4,4,2,192,256]{4,3,2,1,0:T(8,128)} %copy.13.spectra_ref, bf16[4,256,512]{2,1,0:T(8,128)(2,1)} %get-tuple-element.12.inverse_high, bf16[4,256,512]{2,1,0:T(8,128)(2,1)} %get-tuple-element.11.inverse_low, ...), custom_call_target="tpu_custom_call" | custom-call | tf_op jit(solution)/shard_map/pallas_call | solution.py:285
  69.4 232.5 %shard_map.47 = f32[4,2,192,256]{3,2,1,0:T(8,128)} custom-call(s32[8]{0:T(128)} %pivot_ref.1, bf16[8,4,256,512]{3,2,1,0:T(8,128)(2,1)} %get-tuple-element.8.high_ref, bf16[8,4,256,512]{3,2,1,0:T(8,128)(2,1)} %get-tuple-element.9.low_ref, f32[4,2,192,256]{3,2,1,0:T(8,128)} %get-tuple-element.10.start_ref), custom_call_target="tpu_custom_call" | custom-call | tf_op jit(solution)/shard_map/pallas_call | solution.py:323
  301.8 2.7 copy.27
  (1 shorter events, 0.0 us)

commit v2 on v1

--- a/solution.py
+++ b/solution.py
@@ -173,8 +173,9 @@
                 copy(1, f, jnp.int32(piece), left).wait_send()
 
 
-def exchange(dims, spectra_ref, inverse_high, inverse_low, factor_ref, high_ref, low_ref,
-             start_ref, core_buf, chip_buf, core_send, core_recv, chip_send, chip_recv):
+def exchange(dims, spectra_ref, inverse_ref, factor_ref, high_ref, low_ref, start_ref,
+             inverse_high, inverse_low, core_buf, chip_buf, core_send, core_recv, chip_send,
+             chip_recv):
     freqs, blocks, chips = dims
     cases, width = start_ref.shape[2], start_ref.shape[3]
     me = lax.axis_index("freq")
@@ -217,8 +218,14 @@
             )
         pl.semaphore_wait(barrier, chips)
         for f in range(freqs):
-            for shift in range(1, chips + 1):
+            for shift in range(1, chips):
                 core_copy(lax.rem(chip + shift, chips), f).start()
+        for f in range(freqs):
+            core_copy(chip, f).start()
+        for f in range(freqs):
+            inverse_high[f], inverse_low[f] = split(
+                jnp.concatenate([inverse_ref[f, 0].T, inverse_ref[f, 1].T], axis=1)
+            )
 
     for f in range(freqs):
         @pl.when(step == 1 + f)
@@ -271,13 +278,6 @@
     spectra = jnp.einsum("gn,ncr->gcr", part, time_loads, precision=high)
     spectra = spectra.reshape(owners, local_freqs, 2, all_cases, width)
 
-    inverse = jnp.concatenate(
-        [diag_inverse[:, 0].swapaxes(1, 2), diag_inverse[:, 1].swapaxes(1, 2)], axis=2
-    )
-    rounded = lax.reduce_precision(inverse, 8, 7)
-    inverse_high = rounded.astype(jnp.bfloat16)
-    inverse_low = (inverse - rounded).astype(jnp.bfloat16)
-
     chips = owners // 2
     vmem = pl.BlockSpec(memory_space=pltpu.VMEM)
     block = pl.BlockSpec((1, 1, width, 2 * width), lambda f, k: (k, f, 0, 0))
@@ -290,11 +290,13 @@
             jax.ShapeDtypeStruct((local_freqs, 2, all_cases, width), jnp.float32),
         ),
         in_specs=[
-            vmem, vmem, vmem,
+            vmem, vmem,
             pl.BlockSpec((1, 2, width, width), lambda f, k: (f, 0, 0, k)),
         ],
         out_specs=(block, block, vmem),
         scratch_shapes=[
+            pltpu.VMEM((local_freqs, width, 2 * width), jnp.bfloat16),
+            pltpu.VMEM((local_freqs, width, 2 * width), jnp.bfloat16),
             pltpu.VMEM((chips, local_freqs, 2, all_cases, width), jnp.float32),
             pltpu.VMEM((max(chips - 1, 1), local_freqs, 2, all_cases, width), jnp.float32),
             pltpu.SemaphoreType.DMA((chips, local_freqs)),
@@ -306,7 +308,7 @@
             collective_id=1, has_side_effects=True, vmem_limit_bytes=60 * 1024 * 1024,
             dimension_semantics=("arbitrary", "arbitrary"),
         ),
-    )(spectra, inverse_high, inverse_low, factor)
+    )(spectra, diag_inverse, factor)
 
     cases = 8
     while -(-all_cases // (cases + 8)) >= blocks:

time: 305 us -> 301 us (0.987)
  no operation moved by 1% of the time
where the time goes in v2:
time: 301 us
  Pallas kernels  277 us (92%)
  matrix products  16.6 us (6%)
  local copies, waits for them, and re-layouts  6.41 us (2%)
    pallas_call x1, Pallas kernels, body(): pl.pallas_call(functools.partial(substitute, dims), out_shape=jax.ShapeDt...  232 us
    pallas_call x1, Pallas kernels, body(): pl.pallas_call(functools.partial(exchange, (local_freqs, blocks, chips)),...  45 us
    dot_general x1, matrix products, body(): spectra = jnp.einsum('gn,ncr->gcr', part, time_loads, precision=high)  16.6 us

profile of v2, /device:TPU:0, one launch (start us, length us, event | category | flops | bytes accessed | tf_op | source)
XLA Modules:
  0.0 300.5 jit_solution(7274709921988868067)
XLA Ops:
  0.0 0.1 negate_multiply_fusion
  0.1 0.1 fusion.3
  0.2 16.6 %fusion = f32[4,4,2,192,256]{4,1,3,2,0:T(4,128)S(1)} fusion(f32[64,192,256,1,1]{2,1,0,4,3:T(8,128)} %bitcast.5, f32[4,4,2,64,1]{3,1,0,2,4:T(4,128)S(1)} %bitcast.4), kind=kOutput, calls=%fused_computation | convolution fusion | flops 603979776 | bytes 18882560 | tf_op jit(solution)/shard_map/gn,ncr->gcr/dot_general | solution.py:278
  16.8 3.8 %copy.9.spectra_ref = f32[4,4,2,192,256]{4,3,2,1,0:T(8,128)} copy(f32[4,4,2,192,256]{4,1,3,2,0:T(4,128)S(1)} %fusion) | data formatting | bytes 12582912 | tf_op jit(solution)/shard_map/gn,ncr->gcr/dot_general | solution.py:278
  20.5 45.0 %shard_map.46 = (bf16[8,4,256,512]{3,2,1,0:T(8,128)(2,1)}, bf16[8,4,256,512]{3,2,1,0:T(8,128)(2,1)}, f32[4,2,192,256]{3,2,1,0:T(8,128)}) custom-call(f32[4,4,2,192,256]{4,3,2,1,0:T(8,128)} %copy.9.spectra_ref, f32[4,2,256,256]{3,2,1,0:T(8,128)} %inverse_ref.1, f32[4,2,256,2048]{3,2,1,0:T(8,128)} %factor_ref.1), custom_call_target="tpu_custom_call" | custom-call | tf_op jit(solution)/shard_map/pallas_call | solution.py:285
  65.5 232.3 %shard_map.47 = f32[4,2,192,256]{3,2,1,0:T(8,128)} custom-call(s32[8]{0:T(128)} %pivot_ref.1, bf16[8,4,256,512]{3,2,1,0:T(8,128)(2,1)} %get-tuple-element.8.high_ref, bf16[8,4,256,512]{3,2,1,0:T(8,128)(2,1)} %get-tuple-element.9.low_ref, f32[4,2,192,256]{3,2,1,0:T(8,128)} %get-tuple-element.10.start_ref), custom_call_target="tpu_custom_call" | custom-call | tf_op jit(solution)/shard_map/pallas_call | solution.py:325
  297.9 2.7 copy.21
  (1 shorter events, 0.0 us)
